TPU v7x, 128 devices: a whole 4x4x4 slice. The times are simulated.
128 devices in a mesh: chan: 2 (over core), row: 8 (over x_hi, y), col: 8 (over z, x_lo).
Axes of the slice: x: 4 (x_hi: 2, x_lo: 2; x = x_hi * 2 + x_lo), y: 4, z: 4, core: 2. Of those that a mesh axis runs over, the one named last changes fastest.
Arguments:
- pair_acts: bfloat16 [128, 1024, 1024], P('chan', 'row', 'col'), may hold values from -6 to 6
- residue_mask: int32 [1024], replicated, may hold values 0 or 1
- norm_in_gain: float32 [128], replicated, may hold values from 0.1 to 1.9
- w_proj: bfloat16 [5, 128, 128], P(None, 'chan'), may hold values from -0.5 to 0.5
- norm_out_gain: float32 [128], replicated, may hold values from 0.1 to 1.9
- w_out: bfloat16 [128, 128], P('chan'), may hold values from -0.5 to 0.5
Outputs:
- update: bfloat16 [128, 1024, 1024], P('chan', 'row', 'col')
All inputs are finite; a program needn't handle non-finite values.
Results may differ from a plain program's by a relative error of at most 0.0082.
Values may be sent and summed in bfloat16 or wider, within the bound.
A program may use at most 128 MiB of HBM per device.

v0:
```python
import jax
import jax.numpy as jnp
from jax import lax
from jax.sharding import PartitionSpec as P


def normalize(values, gain_vector):
    center = jnp.mean(values, axis=0, keepdims=True)
    spread = jnp.mean(jnp.square(values - center), axis=0, keepdims=True)
    shaped = gain_vector.reshape((-1,) + (1,) * (values.ndim - 1))
    return (values - center) * lax.rsqrt(spread + 1e-05) * shaped


def body(pair_acts, residue_mask, norm_in_gain, w_proj, norm_out_gain, w_out):
    own_channels = pair_acts.shape[0]
    tile_size = pair_acts.shape[1]
    whole_pair = lax.all_gather(pair_acts, "chan", axis=0, tiled=True)
    total_channels = whole_pair.shape[0]
    normed = normalize(whole_pair.astype(jnp.float32), norm_in_gain).astype(jnp.bfloat16)
    normed = normed.reshape(total_channels, tile_size * tile_size)

    def project(proj_index):
        return jnp.dot(w_proj[proj_index], normed, preferred_element_type=jnp.float32)

    row_place = lax.axis_index("row")
    col_place = lax.axis_index("col")
    row_mask = lax.dynamic_slice_in_dim(residue_mask, row_place * tile_size, tile_size).astype(
        jnp.float32
    )
    col_mask = lax.dynamic_slice_in_dim(residue_mask, col_place * tile_size, tile_size).astype(
        jnp.float32
    )
    pair_mask = (row_mask[:, None] * col_mask[None, :]).reshape(-1)
    left_side = (jax.nn.sigmoid(project(0)) * project(1) * pair_mask).astype(jnp.bfloat16)
    left_side = left_side.reshape(own_channels, tile_size, tile_size)
    right_side = (jax.nn.sigmoid(project(2)) * project(3) * pair_mask).astype(jnp.bfloat16)
    right_side = right_side.reshape(own_channels, tile_size, tile_size)
    right_columns = lax.all_gather(right_side, "row", axis=1, tiled=True)
    right_rows = lax.all_to_all(right_columns, "col", split_axis=1, concat_axis=2, tiled=True)
    left_rows = lax.all_gather(left_side, "col", axis=2, tiled=True)
    product = jnp.einsum("cik,cjk->cij", left_rows, right_rows, preferred_element_type=jnp.float32)
    product = product.astype(jnp.bfloat16)
    full_product = lax.all_gather(product, "chan", axis=0, tiled=True)
    normed_out = normalize(full_product.astype(jnp.float32), norm_out_gain).astype(jnp.bfloat16)
    normed_out = normed_out.reshape(total_channels, tile_size * tile_size)
    mixed_out = jnp.dot(w_out, normed_out, preferred_element_type=jnp.float32)
    result = (jax.nn.sigmoid(project(4)) * mixed_out).astype(jnp.bfloat16)
    return result.reshape(own_channels, tile_size, tile_size)


def solution(mesh):
    return jax.shard_map(
        body,
        mesh=mesh,
        in_specs=(P("chan", "row", "col"), P(), P(), P(None, "chan", None), P(), P("chan", None)),
        out_specs=P("chan", "row", "col"),
        check_vma=False,
    )
```

profile of v0, /device:TPU:1, one launch (start us, length us, event | category | flops | bytes accessed | tf_op | source)
XLA Modules:
  0.0 775.5 jit_solution(12208650057472119543)
XLA Ops:
  7.3 0.8 dynamic-slice_convert_fusion.1
  8.3 20.8 %all-gather.5.cloned.1.call-done = bf16[128,128,128]{2,1,0:T(8,128)(2,1)} async-done(((bf16[64,128,128]{2,1,0:T(8,128)(2,1)}), bf16[128,128,128]{2,1,0:T(8,128)(2,1)}) %all-gather.5.cloned.1.call-update) | async-done | bytes 4194320 | tf_op jit(solution)/shard_map/all_gather | solution.py:17
  29.0 3.0 convert_reduce_fusion.1
  32.5 1.1 fusion.21
  33.6 1.4 fusion.23
  35.1 3.3 fusion.13
  38.3 3.1 fusion.42
  41.4 1.9 copy.50
  43.7 5.6 fusion.12
  49.2 3.0 fusion.39
  52.3 1.9 copy.14
  54.3 171.6 %all-gather.9.cloned.1.call-done = bf16[64,1024,128]{2,0,1:T(8,128)(2,1)} async-done(((bf16[64,128,128]{2,0,1:T(8,128)(2,1)}), bf16[64,1024,128]{2,0,1:T(8,128)(2,1)}) %all-gather.9.cloned.1.call-update) | async-done | bytes 16777232 | tf_op jit(solution)/shard_map/all_gather | solution.py:38
  225.9 360.2 %all_to_all.18 = bf16[64,1024,128]{2,0,1:T(8,128)(2,1)S(1)} all-to-all(bf16[64,1024,128]{2,0,1:T(8,128)(2,1)} %all-gather.9.cloned.1.call-done), channel_id=1, replica_groups=mesh['chan'=2,'row'=8,'col'=8] {'col'}, dimensions={1} | all-to-all | bytes 33554432 | tf_op jit(solution)/shard_map/all_to_all | solution.py:39
  586.1 36.0 %copy.49 = bf16[64,8,128,128]{3,1,2,0:T(8,128)(2,1)} copy(bf16[64,8,128,128]{3,0,2,1:T(8,128)(2,1)S(1)} %bitcast.62) | data formatting | bytes 33554432 | tf_op jit(solution)/shard_map/all_to_all | solution.py:39
  622.1 25.4 %all_to_all.16 = bf16[64,128,1024]{2,1,0:T(8,128)(2,1)} reshape(bf16[64,128,8,128]{3,2,1,0:T(8,128)(2,1)} %bitcast.63) | data formatting | bytes 33554432 | tf_op jit(solution)/shard_map/all_to_all | solution.py:39
  647.5 80.0 %all-gather.7.cloned.1.call-done = bf16[64,128,1024]{2,1,0:T(8,128)(2,1)} async-done(((bf16[64,128,128]{2,1,0:T(8,128)(2,1)}), bf16[64,128,1024]{2,1,0:T(8,128)(2,1)}) %all-gather.7.cloned.1.call-update) | async-done | bytes 16777232 | tf_op jit(solution)/shard_map/all_gather | solution.py:40
  727.4 14.4 %convolution_convert_fusion = bf16[64,128,128]{2,1,0:T(8,128)(2,1)} fusion(bf16[64,128,1024]{2,1,0:T(8,128)(2,1)} %all-gather.7.cloned.1.call-done, bf16[64,128,1024]{2,1,0:T(8,128)(2,1)} %all_to_all.16), kind=kOutput, calls=%fused_computation.48 | convolution fusion | flops 2148532224 | bytes 35651584 | tf_op jit(solution)/shard_map/cik,cjk->cij/dot_general | solution.py:41
  741.9 7.4 fusion.11
  749.3 8.0 %all-gather.11.cloned.1.call-done = bf16[128,128,128]{2,1,0:T(8,128)(2,1)} async-done(((bf16[64,128,128]{2,1,0:T(8,128)(2,1)}), bf16[128,128,128]{2,1,0:T(8,128)(2,1)}) %all-gather.11.cloned.1.call-update) | async-done | bytes 4194320 | tf_op jit(solution)/shard_map/all_gather | solution.py:43
  757.3 3.0 convert_reduce_fusion
  760.7 1.1 fusion.18
  761.9 1.4 fusion.20
  764.1 3.0 fusion.36
  767.1 1.9 copy.16
  (31 shorter events, 2.9 us)
Async XLA Ops:
  6.5 756.8 %copy-start = (bf16[64,128]{1,0:T(8,128)(2,1)S(1)}, bf16[64,128]{1,0:T(8,128)(2,1)}, u32[]{:S(2)}) copy-start(bf16[64,128]{1,0:T(8,128)(2,1)} %param.11) | copy-start | bytes 49156
  6.5 22.5 %all-gather.5.cloned.1.call-start = ((), (), s32[]{:S(2)}) async-start(), calls=%async_computation.1 | async-start | bytes 6291456 | tf_op jit(solution)/shard_map/all_gather | solution.py:17
  7.3 218.6 %all-gather.9.cloned.1.call-start = ((), (), s32[]{:S(2)}) async-start(), calls=%async_computation.3 | async-start | bytes 18874368 | tf_op jit(solution)/shard_map/all_gather | solution.py:38
  8.2 25.4 %copy-start.7 = (f32[128]{0:T(128)S(1)}, f32[128]{0:T(128)}, u32[]{:S(2)}) copy-start(f32[128]{0:T(128)} %param.8) | copy-start | bytes 1540
  29.0 3.4 copy-start.3
  33.6 1.4 copy-start.6
  35.0 3.3 copy-start.1
  43.4 684.0 %all-gather.7.cloned.1.call-start = ((), (), s32[]{:S(2)}) async-start(), calls=%async_computation.2 | async-start | bytes 18874368 | tf_op jit(solution)/shard_map/all_gather | solution.py:40
  43.6 5.6 copy-start.2
  54.2 703.1 %all-gather.11.cloned.1.call-start = ((), (), s32[]{:S(2)}) async-start(), calls=%async_computation.4 | async-start | bytes 6291456 | tf_op jit(solution)/shard_map/all_gather | solution.py:43
  749.3 12.6 %copy-start.8 = (f32[128]{0:T(128)S(1)}, f32[128]{0:T(128)}, u32[]{:S(2)}) copy-start(f32[128]{0:T(128)} %param.10) | copy-start | bytes 1540
  757.3 3.4 copy-start.4
  761.9 2.2 copy-start.5
Sparse Core Ops, SparseCore 0:
  9.0 19.9 all-gather.4
  43.5 182.2 all-gather.8
  227.4 499.9 all-gather.6
  742.0 15.2 all-gather.10
where the time goes:
time: 776 us; the launch traced here: 775 us
  blocking collectives  360 us (46%)
  waiting for transfers between devices  281 us (36%)
  local copies, waits for them, and re-layouts  68.9 us (9%)
  matrix products  39.7 us (5%)
  between operations  13.3 us (2%)
  other arithmetic  12 us (2%)
    all_to_all x1, blocking collectives, body(): lax.all_to_all(right_columns, 'col', split_axis=1, concat_axis=2, tiled=T...  360 us
    all_gather x1, waiting for transfers between devices, body(): right_columns = lax.all_gather(right_side, 'row', axis=1, tiled=True)  172 us
    all_gather x1, waiting for transfers between devices, body(): left_rows = lax.all_gather(left_side, 'col', axis=2, tiled=True)  80 us
    all_to_all x2, local copies, waits for them, and re-layouts, body(): lax.all_to_all(right_columns, 'col', split_axis=1, concat_axis=2, tiled=T...  61.4 us
    dot_general x5, matrix products, project(): jnp.dot(w_proj[proj_index], normed, preferred_element_type=jnp.float32)  22.4 us
    all_gather x1, waiting for transfers between devices, body(): whole_pair = lax.all_gather(pair_acts, 'chan', axis=0, tiled=True)  20.8 us
  transfers between devices with their start and end apart: 4, of which 4 were waited for; matrix products, arithmetic and copies ran while one was open for 7% of the time, Pallas kernels for 0%

commit v1 on v0

v1 whole, which is shorter than its diff:
```python
import functools

import jax
import jax.numpy as jnp
from jax import lax
from jax.experimental import pallas as pl
from jax.experimental.pallas import tpu as pltpu
from jax.sharding import PartitionSpec as P

MESH = pl.DeviceIdType.MESH
BF16 = jnp.bfloat16
F32 = jnp.float32


def normalize(values, gain_vector):
    center = jnp.mean(values, axis=0, keepdims=True)
    spread = jnp.mean(jnp.square(values - center), axis=0, keepdims=True)
    shaped = gain_vector.reshape((-1,) + (1,) * (values.ndim - 1))
    return (values - center) * lax.rsqrt(spread + 1e-05) * shaped


def place():
    row, col = lax.axis_index("row"), lax.axis_index("col")
    return lax.axis_index("chan"), (row // 4) * 2 + col % 2, row % 4, col // 2


def device(h, x, y, z):
    return (h, (x // 2) * 4 + y, z * 2 + x % 2)


def offset(q, x, y, z):
    return (x + q // 16) % 4, (y + (q // 4) % 4) % 4, (z + q % 4) % 4


def exchange_kernel(left_ref, right_ref, out_ref, lbuf, rbuf, pbuf, lsend, lrecv, rsend, rrecv, psend, precv, own, xsend, xrecv):
    h, x, y, z = place()
    row, col = lax.axis_index("row"), lax.axis_index("col")
    me = (x * 4 + y) * 4 + z
    barrier = pltpu.get_barrier_semaphore()

    def greet(q, carry):
        pl.semaphore_signal(barrier, inc=1, device_id=device(h, *offset(q, x, y, z)), device_id_type=MESH)
        return carry

    lax.fori_loop(1, 64, greet, 0)
    pl.semaphore_signal(barrier, inc=1, device_id=device(1 - h, x, y, z), device_id_type=MESH)
    pl.semaphore_wait(barrier, 64)

    rows, cols = pl.ds(pl.multiple_of(row * 128, 128), 128), pl.ds(pl.multiple_of(col * 128, 128), 128)

    def scatter(source, target, send_sem, recv_sem):
        def send(o, carry):
            q = (o * 27) % 64
            tx, ty, tz = offset(q, x, y, z)
            pltpu.make_async_remote_copy(
                src_ref=source.at[(tx * 4 + ty) * 4 + tz],
                dst_ref=target.at[rows, cols],
                send_sem=send_sem,
                recv_sem=recv_sem,
                device_id=device(h, tx, ty, tz),
                device_id_type=MESH,
            ).start()
            return carry

        lax.fori_loop(1, 64, send, 0)

    scatter(right_ref, rbuf, rsend, rrecv)
    scatter(left_ref, lbuf, lsend, lrecv)
    copy_l = pltpu.make_async_copy(left_ref.at[me], lbuf.at[rows, cols], own.at[0])
    copy_r = pltpu.make_async_copy(right_ref.at[me], rbuf.at[rows, cols], own.at[1])
    copy_l.start()
    copy_r.start()
    copy_l.wait()
    copy_r.wait()

    def all_of(send_sem, recv_sem):
        return pltpu.make_async_remote_copy(
            src_ref=left_ref.at[pl.ds(0, 63)],
            dst_ref=pbuf.at[pl.ds(0, 63)],
            send_sem=send_sem,
            recv_sem=recv_sem,
            device_id=device(h, *offset(1, x, y, z)),
            device_id_type=MESH,
        )

    all_of(rsend, rrecv).wait()
    all_of(lsend, lrecv).wait()

    def product_rows(t, carry):
        r = (row + t) % 8
        for half in range(2):
            tile = lax.dot_general(
                lbuf[pl.ds(pl.multiple_of(r * 128, 128), 128), :],
                rbuf[half * 512 : half * 512 + 512, :],
                (((1,), (1,)), ((), ())),
                preferred_element_type=F32,
            ).astype(BF16)
            for c in range(4):
                pbuf[r * 8 + half * 4 + c] = tile[:, c * 128 : c * 128 + 128]

        def send(u, inner):
            c = (col + u) % 8

            @pl.when(jnp.logical_or(r != row, c != col))
            def _():
                pltpu.make_async_remote_copy(
                    src_ref=pbuf.at[r * 8 + c],
                    dst_ref=out_ref.at[h * 64 + me],
                    send_sem=psend,
                    recv_sem=precv,
                    device_id=(h, r, c),
                    device_id_type=MESH,
                ).start()

            return inner

        lax.fori_loop(0, 8, send, 0)
        return carry

    lax.fori_loop(0, 8, product_rows, 0)
    copy_p = pltpu.make_async_copy(pbuf.at[row * 8 + col], out_ref.at[h * 64 + me], own.at[0])
    copy_p.start()
    copy_p.wait()
    all_of(psend, precv).wait()
    swap = pltpu.make_async_remote_copy(
        src_ref=out_ref.at[pl.ds(h * 64, 64)],
        dst_ref=out_ref.at[pl.ds(h * 64, 64)],
        send_sem=xsend,
        recv_sem=xrecv,
        device_id=device(1 - h, x, y, z),
        device_id_type=MESH,
    )
    swap.start()
    swap.wait()


def exchange(left_side, right_side):
    vmem = pl.BlockSpec(memory_space=pltpu.VMEM)
    dma = pltpu.SemaphoreType.DMA
    return pl.pallas_call(
        exchange_kernel,
        out_shape=jax.ShapeDtypeStruct((128, 128, 128), BF16),
        in_specs=[vmem, vmem],
        out_specs=vmem,
        scratch_shapes=[
            pltpu.VMEM((1024, 1024), BF16),
            pltpu.VMEM((1024, 1024), BF16),
            pltpu.VMEM((64, 128, 128), BF16),
            dma,
            dma,
            dma,
            dma,
            dma,
            dma,
            dma((2,)),
            dma,
            dma,
        ],
        compiler_params=pltpu.CompilerParams(collective_id=1, has_side_effects=True, vmem_limit_bytes=48 << 20),
        name="triangle",
    )(left_side, right_side)


def body(pair_acts, residue_mask, norm_in_gain, w_proj, norm_out_gain, w_out):
    own_channels = pair_acts.shape[0]
    tile_size = pair_acts.shape[1]
    whole_pair = lax.all_gather(pair_acts, "chan", axis=0, tiled=True)
    total_channels = whole_pair.shape[0]
    normed = normalize(whole_pair.astype(F32), norm_in_gain).astype(BF16)
    normed = normed.reshape(total_channels, tile_size * tile_size)

    def project(proj_index):
        return jnp.dot(w_proj[proj_index], normed, preferred_element_type=F32)

    row_place = lax.axis_index("row")
    col_place = lax.axis_index("col")
    row_mask = lax.dynamic_slice_in_dim(residue_mask, row_place * tile_size, tile_size).astype(F32)
    col_mask = lax.dynamic_slice_in_dim(residue_mask, col_place * tile_size, tile_size).astype(F32)
    pair_mask = (row_mask[:, None] * col_mask[None, :]).reshape(-1)
    left_side = (jax.nn.sigmoid(project(0)) * project(1) * pair_mask).astype(BF16)
    left_side = left_side.reshape(own_channels, tile_size, tile_size)
    right_side = (jax.nn.sigmoid(project(2)) * project(3) * pair_mask).astype(BF16)
    right_side = right_side.reshape(own_channels, tile_size, tile_size)
    full_product = exchange(left_side, right_side)
    normed_out = normalize(full_product.astype(F32), norm_out_gain).astype(BF16)
    normed_out = normed_out.reshape(total_channels, tile_size * tile_size)
    mixed_out = jnp.dot(w_out, normed_out, preferred_element_type=F32)
    result = (jax.nn.sigmoid(project(4)) * mixed_out).astype(BF16)
    return result.reshape(own_channels, tile_size, tile_size)


def solution(mesh):
    return jax.shard_map(
        body,
        mesh=mesh,
        in_specs=(P("chan", "row", "col"), P(), P(), P(None, "chan", None), P(), P("chan", None)),
        out_specs=P("chan", "row", "col"),
        check_vma=False,
    )
```

time: 776 us -> 165 us (0.21)
  blocking collectives: 360 us -> 0 us
  waiting for transfers between devices: 281 us -> 21.5 us
  Pallas kernels: 0 us -> 91.7 us
  local copies, waits for them, and re-layouts: 68.9 us -> 3.97 us
  matrix products: 39.7 us -> 19.1 us
    all_to_all x1 -> x0, blocking collectives: 360 us -> none  [body(): lax.all_to_all(right_columns, 'col', split_axis=1, concat_axis=2, tiled=T...]
    all_gather x3 -> x0, waiting for transfers between devices: 260 us -> none  [the longest x1 172 us: body(): right_columns = lax.all_gather(right_side, 'row', axis=1, tiled=True)]
    pallas_call x0 -> x1, Pallas kernels: none -> 91.7 us  [exchange(): pl.pallas_call(exchange_kernel, out_shape=jax.ShapeDtypeStruct((128, 128,...]
    all_to_all x2 -> x0, local copies, waits for them, and re-layouts: 61.4 us -> none  [body(): lax.all_to_all(right_columns, 'col', split_axis=1, concat_axis=2, tiled=T...]
    dot_general x7 -> x6, matrix products: 39.7 us -> 19.1 us  [the longest x5 16.1 us: project(): return jnp.dot(w_proj[proj_index], normed, preferred_element_type=F32)]
  transfers between devices with their start and end apart: 4 -> 1, of which waited for: 4 -> 1; matrix products, arithmetic and copies ran while one was open for 7% -> 1% of each run, Pallas kernels for 0% -> 0%
where the time goes in v1:
time: 165 us; the launch traced here: 162 us
  Pallas kernels  91.7 us (56%)
  waiting for transfers between devices  21.5 us (13%)
  matrix products  19.1 us (12%)
  between operations  13.6 us (8%)
  other arithmetic  12 us (7%)
  local copies, waits for them, and re-layouts  3.97 us (2%)
    pallas_call x1, Pallas kernels, exchange(): pl.pallas_call(exchange_kernel, out_shape=jax.ShapeDtypeStruct((128, 128,...  91.7 us
    all_gather x1, waiting for transfers between devices, body(): whole_pair = lax.all_gather(pair_acts, 'chan', axis=0, tiled=True)  20.8 us
    dot_general x5, matrix products, project(): return jnp.dot(w_proj[proj_index], normed, preferred_element_type=F32)  16.1 us
    reduce_sum x2, other arithmetic, normalize(): center = jnp.mean(values, axis=0, keepdims=True)  5.96 us
    unnamed x15, local copies, waits for them, and re-layouts  3.97 us
  transfers between devices with their start and end apart: 1, of which 1 were waited for; matrix products, arithmetic and copies ran while one was open for 1% of the time, Pallas kernels for 0%

profile of v1, /device:TPU:1, one launch (start us, length us, event | category | flops | bytes accessed | tf_op | source)
XLA Modules:
  0.0 161.8 jit_solution(8582664250882618419)
XLA Ops:
  6.5 0.7 all-gather.2.cloned.1.call-update
  7.3 0.8 dynamic-slice_convert_fusion.1
  8.1 0.1 multiply_bitcast_fusion
  8.2 0.0 copy-start.4
  8.2 20.8 %all-gather.2.cloned.1.call-done = bf16[128,128,128]{2,1,0:T(8,128)(2,1)} async-done(((bf16[64,128,128]{2,1,0:T(8,128)(2,1)}), bf16[128,128,128]{2,1,0:T(8,128)(2,1)}) %all-gather.2.cloned.1.call-update) | async-done | bytes 4194320 | tf_op jit(solution)/shard_map/all_gather | solution.py:167
  29.0 3.0 %convert_reduce_fusion.1 = f32[128,128]{1,0:T(8,128)S(1)} fusion(bf16[128,128,128]{2,1,0:T(8,128)(2,1)} %all-gather.2.cloned.1.call-done), kind=kLoop, calls=%fused_computation.23 | loop fusion | flops 4177920 | bytes 4259840 | tf_op jit(solution)/shard_map/reduce_sum | solution.py:16
  32.0 0.5 copy-done.2
  32.5 1.1 fusion.21
  33.6 0.0 copy-start.3
  33.6 1.4 fusion.23
  35.0 3.2 %fusion.13 = f32[16384,64]{0,1:T(8,128)S(1)} fusion(bf16[16,8,128,128]{3,2,1,0:T(8,128)(2,1)S(1)} %bitcast.54, bf16[5,64,128]{2,1,0:T(8,128)(2,1)S(1)} %copy-done.3), kind=kOutput, calls=%fused_computation.19 | convolution fusion | flops 271581184 | bytes 8404992 | tf_op jit(solution)/shard_map/dot_general | solution.py:173
  38.3 3.2 %fusion.12 = f32[16384,64]{0,1:T(8,128)S(1)} fusion(bf16[16,8,128,128]{3,2,1,0:T(8,128)(2,1)S(1)} %bitcast.55, bf16[5,64,128]{2,1,0:T(8,128)(2,1)S(1)} %copy-done.3), kind=kOutput, calls=%fused_computation.18 | convolution fusion | flops 271581184 | bytes 8404992 | tf_op jit(solution)/shard_map/dot_general | solution.py:173
  41.5 3.4 %fusion.11 = f32[16384,64]{0,1:T(8,128)S(1)} fusion(bf16[16,8,128,128]{3,2,1,0:T(8,128)(2,1)S(1)} %bitcast.56, bf16[5,64,128]{2,1,0:T(8,128)(2,1)S(1)} %copy-done.3), kind=kOutput, calls=%fused_computation.17 | convolution fusion | flops 271581184 | bytes 8404992 | tf_op jit(solution)/shard_map/dot_general | solution.py:173
  45.0 3.0 %fusion.42 = bf16[8,8,128,128]{3,1,2,0:T(8,128)(2,1)S(1)} fusion(f32[16384]{0:T(1024)S(1)} %multiply_bitcast_fusion, f32[16384,64]{0,1:T(8,128)S(1)} %fusion.13, bf16[16,8,128,128]{3,2,1,0:T(8,128)(2,1)S(1)} %bitcast.57, bf16[5,64,128]{2,1,0:T(8,128)(2,1)S(1)} %copy-done.3), kind=kOutput, calls=%fused_computation.48 | convolution fusion | flops 271581184 | bytes 10567680 | tf_op jit(solution)/shard_map/dot_general | solution.py:173
  48.0 0.6 copy.9
  48.6 3.1 %fusion.39 = bf16[8,8,128,128]{3,1,2,0:T(8,128)(2,1)S(1)} fusion(f32[16384]{0:T(1024)S(1)} %multiply_bitcast_fusion, f32[16384,64]{0,1:T(8,128)S(1)} %fusion.12, bf16[16,8,128,128]{3,2,1,0:T(8,128)(2,1)S(1)} %bitcast.58, bf16[5,64,128]{2,1,0:T(8,128)(2,1)S(1)} %copy-done.3), kind=kOutput, calls=%fused_computation.47 | convolution fusion | flops 271581184 | bytes 10567680 | tf_op jit(solution)/shard_map/dot_general | solution.py:173
  51.7 0.6 copy.8
  52.3 91.7 %triangle.1 = bf16[128,128,128]{2,1,0:T(8,128)(2,1)} custom-call(bf16[64,128,128]{2,1,0:T(8,128)(2,1)S(1)} %bitcast.53, bf16[64,128,128]{2,1,0:T(8,128)(2,1)S(1)} %bitcast.52), custom_call_target="tpu_custom_call" | custom-call | tf_op jit(solution)/shard_map/triangle/pallas_call | solution.py:140
  144.1 3.0 %convert_reduce_fusion = f32[128,128]{1,0:T(8,128)S(1)} fusion(bf16[128,128,128]{2,1,0:T(8,128)(2,1)} %triangle.1), kind=kLoop, calls=%fused_computation.21 | loop fusion | flops 4177920 | bytes 4259840 | tf_op jit(solution)/shard_map/reduce_sum | solution.py:16
  147.1 0.4 copy-done.1
  147.5 1.1 fusion.18
  148.6 1.4 fusion.20
  150.1 3.0 %fusion.36 = bf16[8,8,128,128]{3,1,2,0:T(8,128)(2,1)S(1)} fusion(f32[16384,64]{0,1:T(8,128)S(1)} %fusion.11, bf16[64,128]{1,0:T(8,128)(2,1)S(1)} %copy-done, bf16[16,8,128,128]{3,2,1,0:T(8,128)(2,1)S(1)} %bitcast.59), kind=kOutput, calls=%fused_computation.46 | convolution fusion | flops 270532608 | bytes 10502144 | tf_op jit(solution)/shard_map/dot_general | solution.py:187
  153.1 1.9 %copy.11 = bf16[8,8,128,128]{3,2,1,0:T(8,128)(2,1)} copy(bf16[8,8,128,128]{3,1,2,0:T(8,128)(2,1)S(1)} %fusion.36) | data formatting | bytes 4194304
  (13 shorter events, 0.1 us)
Async XLA Ops:
  6.5 143.5 %copy-start = (bf16[64,128]{1,0:T(8,128)(2,1)S(1)}, bf16[64,128]{1,0:T(8,128)(2,1)}, u32[]{:S(2)}) copy-start(bf16[64,128]{1,0:T(8,128)(2,1)} %param.11) | copy-start | bytes 49156
  6.5 22.5 %all-gather.2.cloned.1.call-start = ((), (), s32[]{:S(2)}) async-start(), calls=%async_computation | async-start | bytes 6291456 | tf_op jit(solution)/shard_map/all_gather | solution.py:167
  8.2 25.4 %copy-start.4 = (f32[128]{0:T(128)S(1)}, f32[128]{0:T(128)}, u32[]{:S(2)}) copy-start(f32[128]{0:T(128)} %param.8) | copy-start | bytes 1540
  29.0 3.4 %copy-start.2 = (bf16[128,128,128]{2,1,0:T(8,128)(2,1)S(1)}, bf16[128,128,128]{2,1,0:T(8,128)(2,1)}, u32[]{:S(2)}) copy-start(bf16[128,128,128]{2,1,0:T(8,128)(2,1)} %all-gather.2.cloned.1.call-done) | copy-start | bytes 12582916
  33.6 1.4 copy-start.3
  144.0 3.5 %copy-start.1 = (bf16[128,128,128]{2,1,0:T(8,128)(2,1)S(1)}, bf16[128,128,128]{2,1,0:T(8,128)(2,1)}, u32[]{:S(2)}) copy-start(bf16[128,128,128]{2,1,0:T(8,128)(2,1)} %triangle.1) | copy-start | bytes 12582916
  144.0 4.6 %copy-start.5 = (f32[128]{0:T(128)S(1)}, f32[128]{0:T(128)}, u32[]{:S(2)}) copy-start(f32[128]{0:T(128)} %param.10) | copy-start | bytes 1540
Sparse Core Ops, SparseCore 0:
  9.0 19.9 all-gather.1

commit v2 on v0

v2 whole, which is shorter than its diff:
```python
import functools

import jax
import jax.numpy as jnp
from jax import lax
from jax.experimental import pallas as pl
from jax.experimental.pallas import tpu as pltpu
from jax.sharding import PartitionSpec as P

MESH = pl.DeviceIdType.MESH
BF16 = jnp.bfloat16
F32 = jnp.float32
CHANNELS = 128
OWN = 64
TILE = 128
CHUNKS = 4
STEP = TILE // CHUNKS
GROUP = 16
BLOCK = 8


def place():
    row, col = lax.axis_index("row"), lax.axis_index("col")
    return lax.axis_index("chan"), (row // 4) * 2 + col % 2, row % 4, col // 2


def device(h, x, y, z):
    return (h, (x // 2) * 4 + y, z * 2 + x % 2)


def offset(q, x, y, z):
    return (x + q // 16) % 4, (y + (q // 4) % 4) % 4, (z + q % 4) % 4


def aligned(start, size):
    return pl.ds(pl.multiple_of(start, size), size)


def sigmoid(value):
    return 0.5 * jnp.tanh(0.5 * value) + 0.5


def layer_norm(source, rows, gain, target):
    def total(b, acc):
        return acc + jnp.sum(source[pl.ds(b * BLOCK, BLOCK), rows, :].astype(F32), axis=0)

    zero = jnp.zeros((GROUP, TILE), F32)
    center = lax.fori_loop(0, CHANNELS // BLOCK, total, zero) * (1.0 / CHANNELS)

    def squares(b, acc):
        shifted = source[pl.ds(b * BLOCK, BLOCK), rows, :].astype(F32) - center[None]
        return acc + jnp.sum(shifted * shifted, axis=0)

    spread = lax.fori_loop(0, CHANNELS // BLOCK, squares, zero) * (1.0 / CHANNELS)
    scale = lax.rsqrt(spread + 1e-05)

    def write(b, carry):
        for u in range(BLOCK):
            c = b * BLOCK + u
            target[aligned(c * GROUP, GROUP), :] = (source[c, rows, :].astype(F32) - center) * scale * gain[c]
        return carry

    lax.fori_loop(0, CHANNELS // BLOCK, write, 0)


def two_rows(source, p):
    first = source[pl.ds(2 * p, CHANNELS, stride=GROUP), :].astype(BF16)
    second = source[pl.ds(2 * p + 1, CHANNELS, stride=GROUP), :].astype(BF16)
    return jnp.concatenate([first, second], axis=1)


def put_rows(target, p, value):
    target[pl.ds(2 * p, OWN, stride=GROUP), :] = value[:, :TILE]
    target[pl.ds(2 * p + 1, OWN, stride=GROUP), :] = value[:, TILE:]


def pack(source, target, rows):
    def step(b, carry):
        block = source[aligned(b * BLOCK * GROUP, BLOCK * GROUP), :]
        target[pl.ds(b * BLOCK, BLOCK), rows, :] = block.reshape(BLOCK, GROUP, TILE).astype(BF16)
        return carry

    lax.fori_loop(0, OWN // BLOCK, step, 0)


def kernel(
    pair, mask_s, gain_in, gain_out, mask_v, w_in, w_out, out,
    whole, normed, stage_a, stage_b, left, right, gate, lbuf, rbuf, rturn, pbuf, prod, result,
    own_x, xsend, xrecv, rsend, rrecv, lsend, lrecv, psend, precv, qsend, qrecv, own, done,
):
    h, x, y, z = place()
    row, col = lax.axis_index("row"), lax.axis_index("col")
    me = (x * 4 + y) * 4 + z
    partner = device(1 - h, x, y, z)
    mine = pl.ds(h * OWN, OWN)
    cols = aligned(col * TILE, TILE)

    def rows_of(s):
        return aligned(s * STEP, STEP)

    def load(s):
        return pltpu.make_async_copy(pair.at[:, rows_of(s), :], whole.at[mine, rows_of(s), :], own_x.at[s])

    def swap(s):
        return pltpu.make_async_remote_copy(
            src_ref=pair.at[:, rows_of(s), :],
            dst_ref=whole.at[mine, rows_of(s), :],
            send_sem=xsend.at[s],
            recv_sem=xrecv.at[s],
            device_id=partner,
            device_id_type=MESH,
        )

    for s in range(CHUNKS):
        load(s).start()
    barrier = pltpu.get_barrier_semaphore()
    pl.semaphore_signal(barrier, inc=1, device_id=partner, device_id_type=MESH)

    def greet(q, carry):
        pl.semaphore_signal(barrier, inc=1, device_id=device(h, *offset(q, x, y, z)), device_id_type=MESH)
        return carry

    lax.fori_loop(1, 64, greet, 0)
    pl.semaphore_wait(barrier, 64)
    for s in range(CHUNKS):
        swap(s).start()

    def scatter(source, s, target, send_sem, recv_sem, own_sem):
        def send(o, carry):
            q = (o * 27) % 64
            tx, ty, tz = offset(q, x, y, z)
            pltpu.make_async_remote_copy(
                src_ref=source.at[(tx * 4 + ty) * 4 + tz, rows_of(s), :],
                dst_ref=target,
                send_sem=send_sem,
                recv_sem=recv_sem,
                device_id=device(h, tx, ty, tz),
                device_id_type=MESH,
            ).start()
            return carry

        lax.fori_loop(1, 64, send, 0)
        pltpu.make_async_copy(source.at[me, rows_of(s), :], target, own_sem).start()

    def others(send_sem, recv_sem, size):
        return pltpu.make_async_remote_copy(
            src_ref=left.at[pl.ds(0, 63), pl.ds(0, size), :],
            dst_ref=right.at[pl.ds(0, 63), pl.ds(0, size), :],
            send_sem=send_sem,
            recv_sem=recv_sem,
            device_id=partner,
            device_id_type=MESH,
        )

    def right_target(s):
        return rbuf.at[aligned(row * TILE + s * STEP, STEP), cols]

    def left_target(s):
        return lbuf.at[s, aligned(row * STEP, STEP), cols]

    col_mask = mask_v[pl.ds(col, 1), :].astype(F32)

    def front(s, carry):
        load(s).wait()
        swap(s).wait()

        def group(g, inner):
            first = s * STEP + g * GROUP
            rows = aligned(first, GROUP)
            layer_norm(whole, rows, gain_in, normed)
            for p in range(GROUP // 2):
                i = first + 2 * p
                proj = jnp.dot(w_in[...], two_rows(normed, p), preferred_element_type=F32)
                mask = jnp.concatenate(
                    [col_mask * mask_s[row * TILE + i + e].astype(F32) for e in range(2)], axis=1
                )
                put_rows(stage_a, p, sigmoid(proj[0:64]) * proj[64:128] * mask)
                put_rows(stage_b, p, sigmoid(proj[128:192]) * proj[192:256] * mask)
                opened = sigmoid(proj[256:320])
                gate[i] = opened[:, :TILE]
                gate[i + 1] = opened[:, TILE:]
            pack(stage_b, right, rows)
            pack(stage_a, left, rows)
            return inner

        lax.fori_loop(0, STEP // GROUP, group, 0)
        scatter(right, s, right_target(s), rsend, rrecv, own.at[0, s])
        return carry

    lax.fori_loop(0, CHUNKS, front, 0)

    def send_left(s, carry):
        scatter(left, s, left_target(s), lsend, lrecv.at[s], own.at[1, s])
        return carry

    lax.fori_loop(0, CHUNKS, send_left, 0)

    for s in range(CHUNKS):
        pltpu.make_async_copy(right.at[me, rows_of(s), :], right_target(s), own.at[0, s]).wait()
    others(rsend, rrecv, TILE).wait_recv()
    for b in range(8):
        rturn[:, b * TILE : b * TILE + TILE] = rbuf[b * TILE : b * TILE + TILE, :].T

    def middle(s, carry):
        pltpu.make_async_copy(left.at[me, rows_of(s), :], left_target(s), own.at[1, s]).wait()
        others(lsend, lrecv.at[s], STEP).wait_recv()
        for half in range(2):
            tile = jnp.dot(
                lbuf[s], rturn[:, half * 512 : half * 512 + 512], preferred_element_type=F32
            ).astype(BF16)
            for r in range(8):
                for c in range(4):
                    pbuf[s, r * 8 + half * 4 + c] = tile[r * STEP : r * STEP + STEP, c * TILE : c * TILE + TILE]

        def send(o, inner):
            q = (o * 27) % 64
            tx, ty, tz = offset(q, x, y, z)
            _, r, c = device(h, tx, ty, tz)
            pltpu.make_async_remote_copy(
                src_ref=pbuf.at[s, r * 8 + c],
                dst_ref=prod.at[h * OWN + me, rows_of(s), :],
                send_sem=psend,
                recv_sem=precv.at[s],
                device_id=(h, r, c),
                device_id_type=MESH,
            ).start()
            return inner

        lax.fori_loop(1, 64, send, 0)
        own_product(s).start()
        return carry

    def own_product(s):
        return pltpu.make_async_copy(
            pbuf.at[s, row * 8 + col], prod.at[h * OWN + me, rows_of(s), :], own.at[2, s]
        )

    def swap_product(s):
        return pltpu.make_async_remote_copy(
            src_ref=prod.at[mine, rows_of(s), :],
            dst_ref=prod.at[mine, rows_of(s), :],
            send_sem=qsend.at[s],
            recv_sem=qrecv.at[s],
            device_id=partner,
            device_id_type=MESH,
        )

    def write_out(s):
        return pltpu.make_async_copy(result.at[:, rows_of(s), :], out.at[:, rows_of(s), :], done.at[s])

    lax.fori_loop(0, CHUNKS, middle, 0)

    def back(s, carry):
        @pl.when(s < CHUNKS)
        def _():
            own_product(s).wait()
            others(psend, precv.at[s], STEP).wait_recv()
            swap_product(s).start()

        @pl.when(s > 0)
        def _():
            swap_product(s - 1).wait()

            def group(g, inner):
                first = (s - 1) * STEP + g * GROUP
                rows = aligned(first, GROUP)
                layer_norm(prod, rows, gain_out, normed)
                for p in range(GROUP // 2):
                    i = first + 2 * p
                    mixed = jnp.dot(w_out[...], two_rows(normed, p), preferred_element_type=F32)
                    put_rows(stage_a, p, mixed * jnp.concatenate([gate[i], gate[i + 1]], axis=1))
                pack(stage_a, result, rows)
                return inner

            lax.fori_loop(0, STEP // GROUP, group, 0)
            write_out(s - 1).start()

        return carry

    lax.fori_loop(0, CHUNKS + 1, back, 0)
    others(rsend, rrecv, TILE).wait_send()
    others(lsend, rrecv, TILE).wait_send()
    others(psend, rrecv, TILE).wait_send()
    for s in range(CHUNKS):
        write_out(s).wait()


def body(pair_acts, residue_mask, norm_in_gain, w_proj, norm_out_gain, w_out):
    vmem = pl.BlockSpec(memory_space=pltpu.VMEM)
    smem = pl.BlockSpec(memory_space=pltpu.SMEM)
    hbm = pl.BlockSpec(memory_space=pl.ANY)
    dma = pltpu.SemaphoreType.DMA
    return pl.pallas_call(
        kernel,
        out_shape=jax.ShapeDtypeStruct((OWN, TILE, TILE), BF16),
        in_specs=[hbm, smem, smem, smem, vmem, vmem, vmem],
        out_specs=hbm,
        scratch_shapes=[
            pltpu.VMEM((CHANNELS, TILE, TILE), BF16),
            pltpu.VMEM((CHANNELS * GROUP, TILE), F32),
            pltpu.VMEM((OWN * GROUP, TILE), F32),
            pltpu.VMEM((OWN * GROUP, TILE), F32),
            pltpu.VMEM((OWN, TILE, TILE), BF16),
            pltpu.VMEM((OWN, TILE, TILE), BF16),
            pltpu.VMEM((TILE, OWN, TILE), F32),
            pltpu.VMEM((CHUNKS, 8 * STEP, 8 * TILE), BF16),
            pltpu.VMEM((8 * TILE, 8 * TILE), BF16),
            pltpu.VMEM((8 * TILE, 8 * TILE), BF16),
            pltpu.VMEM((CHUNKS, 64, STEP, TILE), BF16),
            pltpu.VMEM((CHANNELS, TILE, TILE), BF16),
            pltpu.VMEM((OWN, TILE, TILE), BF16),
            dma((CHUNKS,)),
            dma((CHUNKS,)),
            dma((CHUNKS,)),
            dma,
            dma,
            dma,
            dma((CHUNKS,)),
            dma,
            dma((CHUNKS,)),
            dma((CHUNKS,)),
            dma((CHUNKS,)),
            dma((3, CHUNKS)),
            dma((CHUNKS,)),
        ],
        compiler_params=pltpu.CompilerParams(
            collective_id=1, has_side_effects=True, vmem_limit_bytes=56 << 20
        ),
        name="triangle",
    )(
        pair_acts,
        residue_mask,
        norm_in_gain,
        norm_out_gain,
        residue_mask.reshape(8, TILE),
        w_proj.reshape(5 * OWN, CHANNELS),
        w_out,
    )


def solution(mesh):
    return jax.shard_map(
        body,
        mesh=mesh,
        in_specs=(P("chan", "row", "col"), P(), P(), P(None, "chan", None), P(), P("chan", None)),
        out_specs=P("chan", "row", "col"),
        check_vma=False,
    )
```

time: 776 us -> 99.8 us (0.13)
  blocking collectives: 360 us -> 0 us
  waiting for transfers between devices: 281 us -> 0 us
  Pallas kernels: 0 us -> 96.4 us
  local copies, waits for them, and re-layouts: 68.9 us -> 3.16 us
  matrix products: 39.7 us -> 0 us
  between operations: 13.3 us -> 0.01 us
  other arithmetic: 12 us -> 0 us
    all_to_all x1 -> x0, blocking collectives: 360 us -> none  [body(): lax.all_to_all(right_columns, 'col', split_axis=1, concat_axis=2, tiled=T...]
    all_gather x4 -> x0, waiting for transfers between devices: 280 us -> none  [the longest x1 172 us: body(): right_columns = lax.all_gather(right_side, 'row', axis=1, tiled=True)]
    pallas_call x0 -> x1, Pallas kernels: none -> 96.4 us  [body(): pl.pallas_call(kernel, out_shape=jax.ShapeDtypeStruct((OWN, TILE, TILE),...]
    all_to_all x2 -> x0, local copies, waits for them, and re-layouts: 61.4 us -> none  [body(): lax.all_to_all(right_columns, 'col', split_axis=1, concat_axis=2, tiled=T...]
    dot_general x7 -> x0, matrix products: 39.7 us -> none  [the longest x5 22.4 us: project(): jnp.dot(w_proj[proj_index], normed, preferred_element_type=jnp.float32)]
    reduce_sum x4 -> x0, other arithmetic: 8.21 us -> none  [the longest x2 5.95 us: normalize(): center = jnp.mean(values, axis=0, keepdims=True)]
  transfers between devices with their start and end apart: 4 -> 0, of which waited for: 4 -> 0; matrix products, arithmetic and copies ran while one was open for 7% -> 0% of each run, Pallas kernels for 0% -> 0%
where the time goes in v2:
time: 99.8 us; the launch traced here: 99.6 us
  Pallas kernels  96.4 us (97%)
  local copies, waits for them, and re-layouts  3.16 us (3%)
    pallas_call x1, Pallas kernels, body(): pl.pallas_call(kernel, out_shape=jax.ShapeDtypeStruct((OWN, TILE, TILE),...  96.4 us
    unnamed x1, local copies, waits for them, and re-layouts  3.16 us

profile of v2, /device:TPU:1, one launch (start us, length us, event | category | flops | bytes accessed | tf_op | source)
XLA Modules:
  0.0 99.6 jit_solution(17794362061508699871)
XLA Ops:
  0.0 96.4 %triangle.1 = bf16[64,128,128]{2,1,0:T(8,128)(2,1)} custom-call(bf16[64,128,128]{2,1,0:T(8,128)(2,1)} %pair.1, s32[1024]{0:T(1024)} %mask_s.1, f32[128]{0:T(128)} %gain_in.1, f32[128]{0:T(128)} %gain_out.1, s32[8,128]{1,0:T(8,128)} %bitcast.3, bf16[320,128]{1,0:T(8,128)(2,1)} %bitcast.2, bf16[64,128]{1,0:T(8,128)(2,1)} %w_out.1), custom_call_target="tpu_custom_call" | custom-call | tf_op jit(solution)/shard_map/triangle/pallas_call | solution.py:293
  96.4 3.2 %copy.8 = bf16[64,128,128]{2,1,0:T(8,128)(2,1)} copy(bf16[64,128,128]{2,1,0:T(8,128)(2,1)} %triangle.1) | data formatting | bytes 4194304

commit v3 on v0

v3 whole, which is shorter than its diff:
```python
import jax
import jax.numpy as jnp
from jax import lax
from jax.experimental import pallas as pl
from jax.experimental.pallas import tpu as pltpu
from jax.sharding import PartitionSpec as P

LOGICAL = pl.DeviceIdType.LOGICAL
BF16 = jnp.bfloat16
F32 = jnp.float32
CHANNELS = 128
OWN = 64
TILE = 128
GROUP = 16
BLOCK = 8
X_CHUNKS = ((0, 16), (16, 48), (64, 64))
R_CHUNKS = ((0, 16), (16, 32), (48, 32), (80, 48))
L_CHUNKS = ((0, 32), (32, 32), (64, 32), (96, 16), (112, 16))
INNER = [(1, 2), (2, 1), (3, 3), (0, 1), (1, 0), (3, 2), (2, 3), (0, 2), (2, 0), (1, 1), (3, 1), (1, 3), (0, 3), (3, 0), (2, 2), (0, 0)]


def place():
    row, col = lax.axis_index("row"), lax.axis_index("col")
    return lax.axis_index("chan"), (row // 4) * 2 + col % 2, row % 4, col // 2


def peers(visit):
    _, x, y, z = place()
    along_y = [((y + d) % 4) * 8 for d in range(4)]
    along_z = [((z + d) % 4) * 2 for d in range(4)]

    def step(k, carry):
        d = (k + 1) % 4
        t = (x + d) % 4
        base = (t // 2) * 32 + t % 2
        for dy, dz in INNER[:15]:
            visit(base + along_y[dy] + along_z[dz])

        @pl.when(d != 0)
        def _():
            visit(base + along_y[0] + along_z[0])

        return carry

    lax.fori_loop(0, 4, step, 0)


def aligned(start, size):
    return pl.ds(pl.multiple_of(start, GROUP), size)


def sigmoid(value):
    return 0.5 * jnp.tanh(0.5 * value) + 0.5


def layer_norm(source, rows, gain, target):
    def part(b):
        return source[pl.ds(b * BLOCK, BLOCK), rows, :].astype(F32)

    zero = jnp.zeros((BLOCK, GROUP, TILE), F32)
    steps = CHANNELS // BLOCK

    def total(b, acc):
        return acc + part(b)

    center = jnp.sum(lax.fori_loop(0, steps, total, zero, unroll=2), axis=0) * (1.0 / CHANNELS)

    def squares(b, acc):
        shifted = part(b) - center[None]
        return acc + shifted * shifted

    spread = jnp.sum(lax.fori_loop(0, steps, squares, zero, unroll=2), axis=0) * (1.0 / CHANNELS)
    scale = lax.rsqrt(spread + 1e-05)

    def write(b, carry):
        for u in range(BLOCK):
            c = b * BLOCK + u
            target[pl.ds(pl.multiple_of(c * GROUP, GROUP), GROUP), :] = (
                (source[c, rows, :].astype(F32) - center) * scale * gain[c]
            )
        return carry

    lax.fori_loop(0, steps, write, 0, unroll=2)


def two_rows(source, p):
    first = source[pl.ds(2 * p, CHANNELS, stride=GROUP), :].astype(BF16)
    second = source[pl.ds(2 * p + 1, CHANNELS, stride=GROUP), :].astype(BF16)
    return jnp.concatenate([first, second], axis=1)


def put_rows(target, p, value):
    target[pl.ds(2 * p, OWN, stride=GROUP), :] = value[:, :TILE]
    target[pl.ds(2 * p + 1, OWN, stride=GROUP), :] = value[:, TILE:]


def pack(source, target, rows):
    def step(b, carry):
        block = source[pl.ds(pl.multiple_of(b * BLOCK * GROUP, GROUP), BLOCK * GROUP), :]
        target[pl.ds(b * BLOCK, BLOCK), rows, :] = block.reshape(BLOCK, GROUP, TILE).astype(BF16)
        return carry

    lax.fori_loop(0, OWN // BLOCK, step, 0, unroll=2)


def kernel(
    pair, mask_s, gain_in, gain_out, mask_v, w_in, w_out, out,
    whole, normed, stage_a, stage_b, left, right, gate, lbuf, rbuf, rturn, pbuf, prod,
    own_x, xsend, xrecv, rsend, rrecv, lsend, lrecv, psend, precv, qsend, qrecv, own,
):
    h = lax.axis_index("chan")
    row, col = lax.axis_index("row"), lax.axis_index("col")
    me = row * 8 + col
    home = h * OWN
    partner = (1 - h) * OWN + me
    mine = pl.ds(home, OWN)
    cols = pl.ds(pl.multiple_of(col * TILE, TILE), TILE)

    def load(k):
        rows = pl.ds(*X_CHUNKS[k])
        return pltpu.make_async_copy(pair.at[:, rows, :], whole.at[mine, rows, :], own_x.at[k])

    def swap(k):
        rows = pl.ds(*X_CHUNKS[k])
        return pltpu.make_async_remote_copy(
            src_ref=pair.at[:, rows, :],
            dst_ref=whole.at[mine, rows, :],
            send_sem=xsend.at[k],
            recv_sem=xrecv.at[k],
            device_id=partner,
            device_id_type=LOGICAL,
        )

    for k in range(len(X_CHUNKS)):
        load(k).start()
    barrier = pltpu.get_barrier_semaphore()
    pl.semaphore_signal(barrier, inc=1, device_id=partner, device_id_type=LOGICAL)
    peers(lambda t: pl.semaphore_signal(barrier, inc=1, device_id=home + t, device_id_type=LOGICAL))
    pl.semaphore_wait(barrier, 64)
    for k in range(len(X_CHUNKS)):
        swap(k).start()

    def scatter(source, rows, target, send_sem, recv_sem, own_sem):
        def send(t):
            pltpu.make_async_remote_copy(
                src_ref=source.at[t, rows, :],
                dst_ref=target,
                send_sem=send_sem,
                recv_sem=recv_sem,
                device_id=home + t,
                device_id_type=LOGICAL,
            ).start()

        peers(send)
        pltpu.make_async_copy(source.at[me, rows, :], target, own_sem).start()

    def others(send_sem, recv_sem, size):
        return pltpu.make_async_remote_copy(
            src_ref=left.at[pl.ds(0, 63), pl.ds(0, size), :],
            dst_ref=right.at[pl.ds(0, 63), pl.ds(0, size), :],
            send_sem=send_sem,
            recv_sem=recv_sem,
            device_id=partner,
            device_id_type=LOGICAL,
        )

    def right_target(first, size):
        return rbuf.at[aligned(row * TILE + first, size), cols]

    def left_target(first, size):
        return lbuf.at[aligned(first * 8 + row * size, size), cols]

    col_mask = mask_v[pl.ds(col, 1), :].astype(F32)

    def front(g, carry):
        for k, (start, _) in enumerate(X_CHUNKS):

            @pl.when(g * GROUP == start)
            def _():
                load(k).wait()
                swap(k).wait()

        first = g * GROUP
        rows = aligned(first, GROUP)
        layer_norm(whole, rows, gain_in, normed)
        for p in range(GROUP // 2):
            i = first + 2 * p
            proj = jnp.dot(w_in[...], two_rows(normed, p), preferred_element_type=F32)
            mask = jnp.concatenate([col_mask * mask_s[row * TILE + i + e].astype(F32) for e in range(2)], axis=1)
            put_rows(stage_a, p, sigmoid(proj[0:64]) * proj[64:128] * mask)
            put_rows(stage_b, p, sigmoid(proj[128:192]) * proj[192:256] * mask)
            opened = sigmoid(proj[256:320])
            gate[i] = opened[:, :TILE]
            gate[i + 1] = opened[:, TILE:]
        pack(stage_b, right, rows)
        pack(stage_a, left, rows)
        for k, (start, size) in enumerate(R_CHUNKS):

            @pl.when(first + GROUP == start + size)
            def _():
                scatter(right, pl.ds(start, size), right_target(start, size), rsend, rrecv, own.at[0, k])

        return carry

    lax.fori_loop(0, TILE // GROUP, front, 0)
    for k, (start, size) in enumerate(L_CHUNKS):
        scatter(left, pl.ds(start, size), left_target(start, size), lsend, lrecv.at[k], own.at[1, k])

    for k, (start, size) in enumerate(R_CHUNKS):
        pltpu.make_async_copy(right.at[me, pl.ds(start, size), :], right_target(start, size), own.at[0, k]).wait()
    others(rsend, rrecv, TILE).wait_recv()
    for b in range(8):
        rturn[:, b * TILE : b * TILE + TILE] = rbuf[b * TILE : b * TILE + TILE, :].T

    def product_slice(k, t):
        start, size = L_CHUNKS[k]
        return pbuf.at[t, pl.ds(start, size), :]

    def own_product(k):
        rows = pl.ds(*L_CHUNKS[k])
        return pltpu.make_async_copy(product_slice(k, me), prod.at[home + me, rows, :], own.at[2, k])

    def swap_product(k):
        rows = pl.ds(*L_CHUNKS[k])
        return pltpu.make_async_remote_copy(
            src_ref=prod.at[mine, rows, :],
            dst_ref=prod.at[mine, rows, :],
            send_sem=qsend.at[k],
            recv_sem=qrecv.at[k],
            device_id=partner,
            device_id_type=LOGICAL,
        )

    for k, (start, size) in enumerate(L_CHUNKS):
        pltpu.make_async_copy(left.at[me, pl.ds(start, size), :], left_target(start, size), own.at[1, k]).wait()
        others(lsend, lrecv.at[k], size).wait_recv()
        for half in range(2):
            tile = jnp.dot(
                lbuf[start * 8 : (start + size) * 8, :],
                rturn[:, half * 512 : half * 512 + 512],
                preferred_element_type=F32,
            ).astype(BF16)
            for r in range(8):
                for c in range(4):
                    pbuf[r * 8 + half * 4 + c, start : start + size, :] = tile[
                        r * size : r * size + size, c * TILE : c * TILE + TILE
                    ]
        rows = pl.ds(start, size)

        def send(t):
            pltpu.make_async_remote_copy(
                src_ref=product_slice(k, t),
                dst_ref=prod.at[home + me, rows, :],
                send_sem=psend,
                recv_sem=precv.at[k],
                device_id=home + t,
                device_id_type=LOGICAL,
            ).start()

        peers(send)
        own_product(k).start()

    def finish(first):
        rows = aligned(first, GROUP)
        layer_norm(prod, rows, gain_out, normed)
        for p in range(GROUP // 2):
            i = first + 2 * p
            mixed = jnp.dot(w_out[...], two_rows(normed, p), preferred_element_type=F32)
            put_rows(stage_a, p, mixed * jnp.concatenate([gate[i], gate[i + 1]], axis=1))
        pack(stage_a, out, rows)

    for k in range(len(L_CHUNKS) + 1):
        if k < len(L_CHUNKS):
            own_product(k).wait()
            others(psend, precv.at[k], L_CHUNKS[k][1]).wait_recv()
            swap_product(k).start()
        if k > 0:
            swap_product(k - 1).wait()
            start, size = L_CHUNKS[k - 1]

            def group(g, carry):
                finish(start + g * GROUP)
                return carry

            lax.fori_loop(0, size // GROUP, group, 0)
    others(rsend, rrecv, TILE).wait_send()
    others(lsend, rrecv, TILE).wait_send()
    others(psend, rrecv, TILE).wait_send()


def body(pair_acts, residue_mask, norm_in_gain, w_proj, norm_out_gain, w_out):
    vmem = pl.BlockSpec(memory_space=pltpu.VMEM)
    smem = pl.BlockSpec(memory_space=pltpu.SMEM)
    dma = pltpu.SemaphoreType.DMA
    parts = len(L_CHUNKS)
    return pl.pallas_call(
        kernel,
        out_shape=pltpu.VMEM((OWN, TILE, TILE), BF16),
        in_specs=[pl.BlockSpec(memory_space=pl.ANY), smem, smem, smem, vmem, vmem, vmem],
        out_specs=vmem,
        scratch_shapes=[
            pltpu.VMEM((CHANNELS, TILE, TILE), BF16),
            pltpu.VMEM((CHANNELS * GROUP, TILE), F32),
            pltpu.VMEM((OWN * GROUP, TILE), F32),
            pltpu.VMEM((OWN * GROUP, TILE), F32),
            pltpu.VMEM((OWN, TILE, TILE), BF16),
            pltpu.VMEM((OWN, TILE, TILE), BF16),
            pltpu.VMEM((TILE, OWN, TILE), F32),
            pltpu.VMEM((8 * TILE, 8 * TILE), BF16),
            pltpu.VMEM((8 * TILE, 8 * TILE), BF16),
            pltpu.VMEM((8 * TILE, 8 * TILE), BF16),
            pltpu.VMEM((64, TILE, TILE), BF16),
            pltpu.VMEM((CHANNELS, TILE, TILE), BF16),
            dma((len(X_CHUNKS),)),
            dma((len(X_CHUNKS),)),
            dma((len(X_CHUNKS),)),
            dma,
            dma,
            dma,
            dma((parts,)),
            dma,
            dma((parts,)),
            dma((parts,)),
            dma((parts,)),
            dma((3, parts)),
        ],
        compiler_params=pltpu.CompilerParams(collective_id=1, has_side_effects=True, vmem_limit_bytes=56 << 20),
        name="triangle",
    )(
        pair_acts,
        residue_mask,
        norm_in_gain,
        norm_out_gain,
        residue_mask.reshape(8, TILE),
        w_proj.reshape(5 * OWN, CHANNELS),
        w_out,
    )


def solution(mesh):
    return jax.shard_map(
        body,
        mesh=mesh,
        in_specs=(P("chan", "row", "col"), P(), P(), P(None, "chan", None), P(), P("chan", None)),
        out_specs=P("chan", "row", "col"),
        check_vma=False,
    )
```

time: 776 us -> 91.4 us (0.12)
  blocking collectives: 360 us -> 0 us
  waiting for transfers between devices: 281 us -> 0 us
  Pallas kernels: 0 us -> 89.9 us
  local copies, waits for them, and re-layouts: 68.9 us -> 1.32 us
  matrix products: 39.7 us -> 0 us
  between operations: 13.3 us -> 0.01 us
  other arithmetic: 12 us -> 0 us
    all_to_all x1 -> x0, blocking collectives: 360 us -> none  [body(): lax.all_to_all(right_columns, 'col', split_axis=1, concat_axis=2, tiled=T...]
    all_gather x4 -> x0, waiting for transfers between devices: 280 us -> none  [the longest x1 172 us: body(): right_columns = lax.all_gather(right_side, 'row', axis=1, tiled=True)]
    pallas_call x0 -> x1, Pallas kernels: none -> 89.9 us  [body(): pl.pallas_call(kernel, out_shape=pltpu.VMEM((OWN, TILE, TILE), BF16), in_...]
    all_to_all x2 -> x0, local copies, waits for them, and re-layouts: 61.4 us -> none  [body(): lax.all_to_all(right_columns, 'col', split_axis=1, concat_axis=2, tiled=T...]
    dot_general x7 -> x0, matrix products: 39.7 us -> none  [the longest x5 22.4 us: project(): jnp.dot(w_proj[proj_index], normed, preferred_element_type=jnp.float32)]
    reduce_sum x4 -> x0, other arithmetic: 8.21 us -> none  [the longest x2 5.95 us: normalize(): center = jnp.mean(values, axis=0, keepdims=True)]
  transfers between devices with their start and end apart: 4 -> 0, of which waited for: 4 -> 0; matrix products, arithmetic and copies ran while one was open for 7% -> 0% of each run, Pallas kernels for 0% -> 0%
where the time goes in v3:
time: 91.4 us; the launch traced here: 91.2 us
  Pallas kernels  89.9 us (98%)
  local copies, waits for them, and re-layouts  1.32 us (1%)
    pallas_call x1, Pallas kernels, body(): pl.pallas_call(kernel, out_shape=pltpu.VMEM((OWN, TILE, TILE), BF16), in_...  89.9 us

profile of v3, /device:TPU:1, one launch (start us, length us, event | category | flops | bytes accessed | tf_op | source)
XLA Modules:
  0.0 91.2 jit_solution(17770474935246576405)
XLA Ops:
  0.0 89.9 %triangle.1 = bf16[64,128,128]{2,1,0:T(8,128)(2,1)S(1)} custom-call(bf16[64,128,128]{2,1,0:T(8,128)(2,1)} %pair.1, s32[1024]{0:T(1024)} %mask_s.1, f32[128]{0:T(128)} %gain_in.1, f32[128]{0:T(128)} %gain_out.1, s32[8,128]{1,0:T(8,128)} %bitcast.3, bf16[320,128]{1,0:T(8,128)(2,1)} %bitcast.2, bf16[64,128]{1,0:T(8,128)(2,1)} %w_out.1), custom_call_target="tpu_custom_call" | custom-call | tf_op jit(solution)/shard_map/triangle/pallas_call | solution.py:296
  89.9 1.3 %copy.8 = bf16[64,128,128]{2,1,0:T(8,128)(2,1)} copy(bf16[64,128,128]{2,1,0:T(8,128)(2,1)S(1)} %triangle.1) | data formatting | bytes 4194304

commit v4 on v3

--- a/solution.py
+++ b/solution.py
@@ -14,7 +14,7 @@
 GROUP = 16
 BLOCK = 8
 X_CHUNKS = ((0, 16), (16, 48), (64, 64))
-R_CHUNKS = ((0, 16), (16, 32), (48, 32), (80, 48))
+R_CHUNKS = ((0, 16), (16, 16), (32, 32), (64, 32), (96, 32))
 L_CHUNKS = ((0, 32), (32, 32), (64, 32), (96, 16), (112, 16))
 INNER = [(1, 2), (2, 1), (3, 3), (0, 1), (1, 0), (3, 2), (2, 3), (0, 2), (2, 0), (1, 1), (3, 1), (1, 3), (0, 3), (3, 0), (2, 2), (0, 0)]
 
@@ -43,6 +43,16 @@
         return carry
 
     lax.fori_loop(0, 4, step, 0)
+
+
+def greet(visit):
+    _, x, y, z = place()
+    along_x = [(((x + d) % 4) // 2) * 32 + (x + d) % 2 for d in range(4)]
+    along_y = [((y + d) % 4) * 8 for d in range(4)]
+    along_z = [((z + d) % 4) * 2 for d in range(4)]
+    offsets = [(a, b, c) for a in range(4) for b in range(4) for c in range(4)][1:]
+    for a, b, c in sorted(offsets, key=lambda o: -sum(min(d, 4 - d) for d in o)):
+        visit(along_x[a] + along_y[b] + along_z[c])
 
 
 def aligned(start, size):
@@ -104,9 +114,9 @@
 
 
 def kernel(
-    pair, mask_s, gain_in, gain_out, mask_v, w_in, w_out, out,
-    whole, normed, stage_a, stage_b, left, right, gate, lbuf, rbuf, rturn, pbuf, prod,
-    own_x, xsend, xrecv, rsend, rrecv, lsend, lrecv, psend, precv, qsend, qrecv, own,
+    pair, mask_hbm, gain_in_hbm, gain_out_hbm, mask_rows_hbm, w_in_hbm, w_out_hbm, out,
+    mask_s, gain_in, gain_out, mask_v, w_in, w_out, whole, normed, stage_a, stage_b, left, right, gate, lbuf, rbuf, rturn, pbuf, prod,
+    own_x, xsend, xrecv, rsend, rrecv, lsend, lrecv, psend, precv, qsend, qrecv, own, fetched,
 ):
     h = lax.axis_index("chan")
     row, col = lax.axis_index("row"), lax.axis_index("col")
@@ -131,11 +141,24 @@
             device_id_type=LOGICAL,
         )
 
+    barrier = pltpu.get_barrier_semaphore()
+    greet(lambda t: pl.semaphore_signal(barrier, inc=1, device_id=home + t, device_id_type=LOGICAL))
+    pl.semaphore_signal(barrier, inc=1, device_id=partner, device_id_type=LOGICAL)
+    operands = (
+        (mask_hbm, mask_s),
+        (gain_in_hbm, gain_in),
+        (gain_out_hbm, gain_out),
+        (mask_rows_hbm, mask_v),
+        (w_in_hbm, w_in),
+        (w_out_hbm, w_out),
+    )
+    fetches = [pltpu.make_async_copy(src, dst, fetched.at[k]) for k, (src, dst) in enumerate(operands)]
     for k in range(len(X_CHUNKS)):
         load(k).start()
-    barrier = pltpu.get_barrier_semaphore()
-    pl.semaphore_signal(barrier, inc=1, device_id=partner, device_id_type=LOGICAL)
-    peers(lambda t: pl.semaphore_signal(barrier, inc=1, device_id=home + t, device_id_type=LOGICAL))
+    for fetch in fetches:
+        fetch.start()
+    for fetch in fetches:
+        fetch.wait()
     pl.semaphore_wait(barrier, 64)
     for k in range(len(X_CHUNKS)):
         swap(k).start()
@@ -290,15 +313,20 @@
 
 def body(pair_acts, residue_mask, norm_in_gain, w_proj, norm_out_gain, w_out):
     vmem = pl.BlockSpec(memory_space=pltpu.VMEM)
-    smem = pl.BlockSpec(memory_space=pltpu.SMEM)
     dma = pltpu.SemaphoreType.DMA
     parts = len(L_CHUNKS)
     return pl.pallas_call(
         kernel,
         out_shape=pltpu.VMEM((OWN, TILE, TILE), BF16),
-        in_specs=[pl.BlockSpec(memory_space=pl.ANY), smem, smem, smem, vmem, vmem, vmem],
+        in_specs=[pl.BlockSpec(memory_space=pl.ANY)] * 7,
         out_specs=vmem,
         scratch_shapes=[
+            pltpu.SMEM((8 * TILE,), jnp.int32),
+            pltpu.SMEM((CHANNELS,), F32),
+            pltpu.SMEM((CHANNELS,), F32),
+            pltpu.VMEM((8, TILE), jnp.int32),
+            pltpu.VMEM((5 * OWN, CHANNELS), BF16),
+            pltpu.VMEM((OWN, CHANNELS), BF16),
             pltpu.VMEM((CHANNELS, TILE, TILE), BF16),
             pltpu.VMEM((CHANNELS * GROUP, TILE), F32),
             pltpu.VMEM((OWN * GROUP, TILE), F32),
@@ -323,6 +351,7 @@
             dma((parts,)),
             dma((parts,)),
             dma((3, parts)),
+            dma((6,)),
         ],
         compiler_params=pltpu.CompilerParams(collective_id=1, has_side_effects=True, vmem_limit_bytes=56 << 20),
         name="triangle",

time: 91.4 us -> 89.7 us (0.981)
  Pallas kernels: 89.9 us -> 88.3 us
    pallas_call x1, Pallas kernels: 89.9 us -> 88.3 us  [body(): pl.pallas_call(kernel, out_shape=pltpu.VMEM((OWN, TILE, TILE), BF16), in_...]
where the time goes in v4:
time: 89.7 us; the launch traced here: 89.6 us
  Pallas kernels  88.3 us (98%)
  local copies, waits for them, and re-layouts  1.32 us (1%)
    pallas_call x1, Pallas kernels, body(): pl.pallas_call(kernel, out_shape=pltpu.VMEM((OWN, TILE, TILE), BF16), in_...  88.3 us

profile of v4, /device:TPU:1, one launch (start us, length us, event | category | flops | bytes accessed | tf_op | source)
XLA Modules:
  0.0 89.6 jit_solution(13705538829139672343)
XLA Ops:
  0.0 88.3 %triangle.1 = bf16[64,128,128]{2,1,0:T(8,128)(2,1)S(1)} custom-call(bf16[64,128,128]{2,1,0:T(8,128)(2,1)} %pair.1, s32[1024]{0:T(1024)} %mask_hbm.1, f32[128]{0:T(128)} %gain_in_hbm.1, f32[128]{0:T(128)} %gain_out_hbm.1, s32[8,128]{1,0:T(8,128)} %bitcast.3, bf16[320,128]{1,0:T(8,128)(2,1)} %bitcast.2, bf16[64,128]{1,0:T(8,128)(2,1)} %w_out_hbm.1), custom_call_target="tpu_custom_call" | custom-call | tf_op jit(solution)/shard_map/triangle/pallas_call | solution.py:318
  88.3 1.3 %copy.8 = bf16[64,128,128]{2,1,0:T(8,128)(2,1)} copy(bf16[64,128,128]{2,1,0:T(8,128)(2,1)S(1)} %triangle.1) | data formatting | bytes 4194304

commit v5 on v4

--- a/solution.py
+++ b/solution.py
@@ -116,7 +116,7 @@
 def kernel(
     pair, mask_hbm, gain_in_hbm, gain_out_hbm, mask_rows_hbm, w_in_hbm, w_out_hbm, out,
     mask_s, gain_in, gain_out, mask_v, w_in, w_out, whole, normed, stage_a, stage_b, left, right, gate, lbuf, rbuf, rturn, pbuf, prod,
-    own_x, xsend, xrecv, rsend, rrecv, lsend, lrecv, psend, precv, qsend, qrecv, own, fetched,
+    own_x, xsend, xrecv, rsend, rrecv, lsend, lrecv, psend, precv, qsend, qrecv, own, fetched, ready, go,
 ):
     h = lax.axis_index("chan")
     row, col = lax.axis_index("row"), lax.axis_index("col")
@@ -142,8 +142,12 @@
         )
 
     barrier = pltpu.get_barrier_semaphore()
-    greet(lambda t: pl.semaphore_signal(barrier, inc=1, device_id=home + t, device_id_type=LOGICAL))
-    pl.semaphore_signal(barrier, inc=1, device_id=partner, device_id_type=LOGICAL)
+
+    @pl.when(h == 1)
+    def _():
+        pl.semaphore_signal(barrier, inc=1, device_id=partner, device_id_type=LOGICAL)
+
+    greet(lambda t: pl.semaphore_signal(barrier, inc=1, device_id=OWN + t, device_id_type=LOGICAL))
     operands = (
         (mask_hbm, mask_s),
         (gain_in_hbm, gain_in),
@@ -157,11 +161,30 @@
         load(k).start()
     for fetch in fetches:
         fetch.start()
+
+    @pl.when(h == 0)
+    def _():
+        pl.semaphore_wait(barrier, 1)
+        pl.semaphore_signal(ready, inc=1, device_id=partner, device_id_type=LOGICAL)
+
+    @pl.when(h == 1)
+    def _():
+        pl.semaphore_wait(ready, 1)
+
+    for k in range(len(X_CHUNKS)):
+        swap(k).start()
     for fetch in fetches:
         fetch.wait()
-    pl.semaphore_wait(barrier, 64)
-    for k in range(len(X_CHUNKS)):
-        swap(k).start()
+
+    def all_here():
+        @pl.when(h == 1)
+        def _():
+            pl.semaphore_wait(barrier, 126)
+            pl.semaphore_signal(go, inc=1, device_id=partner, device_id_type=LOGICAL)
+
+        @pl.when(h == 0)
+        def _():
+            pl.semaphore_wait(go, 1)
 
     def scatter(source, rows, target, send_sem, recv_sem, own_sem):
         def send(t):
@@ -217,6 +240,11 @@
             gate[i + 1] = opened[:, TILE:]
         pack(stage_b, right, rows)
         pack(stage_a, left, rows)
+
+        @pl.when(g == 0)
+        def _():
+            all_here()
+
         for k, (start, size) in enumerate(R_CHUNKS):
 
             @pl.when(first + GROUP == start + size)
@@ -352,6 +380,8 @@
             dma((parts,)),
             dma((3, parts)),
             dma((6,)),
+            pltpu.SemaphoreType.REGULAR,
+            pltpu.SemaphoreType.REGULAR,
         ],
         compiler_params=pltpu.CompilerParams(collective_id=1, has_side_effects=True, vmem_limit_bytes=56 << 20),
         name="triangle",

time: 89.7 us -> 87.1 us (0.971)
  Pallas kernels: 88.3 us -> 85.7 us
    pallas_call x1, Pallas kernels: 88.3 us -> 85.7 us  [body(): pl.pallas_call(kernel, out_shape=pltpu.VMEM((OWN, TILE, TILE), BF16), in_...]
where the time goes in v5:
time: 87.1 us; the launch traced here: 87 us
  Pallas kernels  85.7 us (98%)
  local copies, waits for them, and re-layouts  1.32 us (2%)
    pallas_call x1, Pallas kernels, body(): pl.pallas_call(kernel, out_shape=pltpu.VMEM((OWN, TILE, TILE), BF16), in_...  85.7 us

profile of v5, /device:TPU:1, one launch (start us, length us, event | category | flops | bytes accessed | tf_op | source)
XLA Modules:
  0.0 87.0 jit_solution(12103753908711049281)
XLA Ops:
  0.0 85.7 %triangle.1 = bf16[64,128,128]{2,1,0:T(8,128)(2,1)S(1)} custom-call(bf16[64,128,128]{2,1,0:T(8,128)(2,1)} %pair.1, s32[1024]{0:T(1024)} %mask_hbm.1, f32[128]{0:T(128)} %gain_in_hbm.1, f32[128]{0:T(128)} %gain_out_hbm.1, s32[8,128]{1,0:T(8,128)} %bitcast.3, bf16[320,128]{1,0:T(8,128)(2,1)} %bitcast.2, bf16[64,128]{1,0:T(8,128)(2,1)} %w_out_hbm.1), custom_call_target="tpu_custom_call" | custom-call | tf_op jit(solution)/shard_map/triangle/pallas_call | solution.py:346
  85.7 1.3 %copy.8 = bf16[64,128,128]{2,1,0:T(8,128)(2,1)} copy(bf16[64,128,128]{2,1,0:T(8,128)(2,1)S(1)} %triangle.1) | data formatting | bytes 4194304

commit v6 on v5

--- a/solution.py
+++ b/solution.py
@@ -14,8 +14,8 @@
 GROUP = 16
 BLOCK = 8
 X_CHUNKS = ((0, 16), (16, 48), (64, 64))
-R_CHUNKS = ((0, 16), (16, 16), (32, 32), (64, 32), (96, 32))
-L_CHUNKS = ((0, 32), (32, 32), (64, 32), (96, 16), (112, 16))
+R_CHUNKS = ((0, 16), (16, 16), (32, 16), (48, 16), (64, 32), (96, 32))
+L_CHUNKS = ((0, 32), (32, 32), (64, 16), (80, 16), (96, 16), (112, 16))
 INNER = [(1, 2), (2, 1), (3, 3), (0, 1), (1, 0), (3, 2), (2, 3), (0, 2), (2, 0), (1, 1), (3, 1), (1, 3), (0, 3), (3, 0), (2, 2), (0, 0)]
 
 
@@ -26,19 +26,18 @@
 
 def peers(visit):
     _, x, y, z = place()
+    along_x = [(((x + d) % 4) // 2) * 32 + (x + d) % 2 for d in range(4)]
     along_y = [((y + d) % 4) * 8 for d in range(4)]
-    along_z = [((z + d) % 4) * 2 for d in range(4)]
 
     def step(k, carry):
         d = (k + 1) % 4
-        t = (x + d) % 4
-        base = (t // 2) * 32 + t % 2
-        for dy, dz in INNER[:15]:
-            visit(base + along_y[dy] + along_z[dz])
+        along_z = [((z + d + e) % 4) * 2 for e in range(4)]
+        for dx, dy in INNER[:15]:
+            visit(along_x[dx] + along_y[dy] + along_z[(8 - dx - dy) % 4])
 
         @pl.when(d != 0)
         def _():
-            visit(base + along_y[0] + along_z[0])
+            visit(along_x[0] + along_y[0] + along_z[0])
 
         return carry
 

time: 87.1 us -> 86.4 us (level)
  no operation moved by 1% of the time
where the time goes in v6:
time: 86.4 us; the launch traced here: 86.2 us
  Pallas kernels  84.9 us (98%)
  local copies, waits for them, and re-layouts  1.32 us (2%)
    pallas_call x1, Pallas kernels, body(): pl.pallas_call(kernel, out_shape=pltpu.VMEM((OWN, TILE, TILE), BF16), in_...  84.9 us

profile of v6, /device:TPU:1, one launch (start us, length us, event | category | flops | bytes accessed | tf_op | source)
XLA Modules:
  0.0 86.2 jit_solution(1047206051825037934)
XLA Ops:
  0.0 84.9 %triangle.1 = bf16[64,128,128]{2,1,0:T(8,128)(2,1)S(1)} custom-call(bf16[64,128,128]{2,1,0:T(8,128)(2,1)} %pair.1, s32[1024]{0:T(1024)} %mask_hbm.1, f32[128]{0:T(128)} %gain_in_hbm.1, f32[128]{0:T(128)} %gain_out_hbm.1, s32[8,128]{1,0:T(8,128)} %bitcast.3, bf16[320,128]{1,0:T(8,128)(2,1)} %bitcast.2, bf16[64,128]{1,0:T(8,128)(2,1)} %w_out_hbm.1), custom_call_target="tpu_custom_call" | custom-call | tf_op jit(solution)/shard_map/triangle/pallas_call | solution.py:345
  84.9 1.3 %copy.8 = bf16[64,128,128]{2,1,0:T(8,128)(2,1)} copy(bf16[64,128,128]{2,1,0:T(8,128)(2,1)S(1)} %triangle.1) | data formatting | bytes 4194304

commit v7 on v6

--- a/solution.py
+++ b/solution.py
@@ -72,13 +72,13 @@
     def total(b, acc):
         return acc + part(b)
 
-    center = jnp.sum(lax.fori_loop(0, steps, total, zero, unroll=2), axis=0) * (1.0 / CHANNELS)
+    center = jnp.sum(lax.fori_loop(0, steps, total, zero, unroll=4), axis=0) * (1.0 / CHANNELS)
 
     def squares(b, acc):
         shifted = part(b) - center[None]
         return acc + shifted * shifted
 
-    spread = jnp.sum(lax.fori_loop(0, steps, squares, zero, unroll=2), axis=0) * (1.0 / CHANNELS)
+    spread = jnp.sum(lax.fori_loop(0, steps, squares, zero, unroll=4), axis=0) * (1.0 / CHANNELS)
     scale = lax.rsqrt(spread + 1e-05)
 
     def write(b, carry):
@@ -89,7 +89,7 @@
             )
         return carry
 
-    lax.fori_loop(0, steps, write, 0, unroll=2)
+    lax.fori_loop(0, steps, write, 0, unroll=4)
 
 
 def two_rows(source, p):
@@ -134,7 +134,7 @@
         return pltpu.make_async_remote_copy(
             src_ref=pair.at[:, rows, :],
             dst_ref=whole.at[mine, rows, :],
-            send_sem=xsend.at[k],
+            send_sem=xsend,
             recv_sem=xrecv.at[k],
             device_id=partner,
             device_id_type=LOGICAL,
@@ -223,7 +223,7 @@
             @pl.when(g * GROUP == start)
             def _():
                 load(k).wait()
-                swap(k).wait()
+                swap(k).wait_recv()
 
         first = g * GROUP
         rows = aligned(first, GROUP)
@@ -248,17 +248,17 @@
 
             @pl.when(first + GROUP == start + size)
             def _():
-                scatter(right, pl.ds(start, size), right_target(start, size), rsend, rrecv, own.at[0, k])
+                scatter(right, pl.ds(start, size), right_target(start, size), rsend, rrecv, own.at[0])
 
         return carry
 
     lax.fori_loop(0, TILE // GROUP, front, 0)
     for k, (start, size) in enumerate(L_CHUNKS):
-        scatter(left, pl.ds(start, size), left_target(start, size), lsend, lrecv.at[k], own.at[1, k])
-
-    for k, (start, size) in enumerate(R_CHUNKS):
-        pltpu.make_async_copy(right.at[me, pl.ds(start, size), :], right_target(start, size), own.at[0, k]).wait()
+        scatter(left, pl.ds(start, size), left_target(start, size), lsend, lrecv.at[k], own.at[1])
+
+    pltpu.make_async_copy(right.at[me], right_target(0, TILE), own.at[0]).wait()
     others(rsend, rrecv, TILE).wait_recv()
+    pltpu.make_async_copy(left.at[me], right_target(0, TILE), own.at[1]).wait()
     for b in range(8):
         rturn[:, b * TILE : b * TILE + TILE] = rbuf[b * TILE : b * TILE + TILE, :].T
 
@@ -268,21 +268,20 @@
 
     def own_product(k):
         rows = pl.ds(*L_CHUNKS[k])
-        return pltpu.make_async_copy(product_slice(k, me), prod.at[home + me, rows, :], own.at[2, k])
+        return pltpu.make_async_copy(product_slice(k, me), prod.at[home + me, rows, :], own.at[2])
 
     def swap_product(k):
         rows = pl.ds(*L_CHUNKS[k])
         return pltpu.make_async_remote_copy(
             src_ref=prod.at[mine, rows, :],
             dst_ref=prod.at[mine, rows, :],
-            send_sem=qsend.at[k],
+            send_sem=qsend,
             recv_sem=qrecv.at[k],
             device_id=partner,
             device_id_type=LOGICAL,
         )
 
     for k, (start, size) in enumerate(L_CHUNKS):
-        pltpu.make_async_copy(left.at[me, pl.ds(start, size), :], left_target(start, size), own.at[1, k]).wait()
         others(lsend, lrecv.at[k], size).wait_recv()
         for half in range(2):
             tile = jnp.dot(
@@ -319,13 +318,13 @@
             put_rows(stage_a, p, mixed * jnp.concatenate([gate[i], gate[i + 1]], axis=1))
         pack(stage_a, out, rows)
 
+    pltpu.make_async_copy(pbuf.at[me], prod.at[home + me], own.at[2]).wait()
     for k in range(len(L_CHUNKS) + 1):
         if k < len(L_CHUNKS):
-            own_product(k).wait()
             others(psend, precv.at[k], L_CHUNKS[k][1]).wait_recv()
             swap_product(k).start()
         if k > 0:
-            swap_product(k - 1).wait()
+            swap_product(k - 1).wait_recv()
             start, size = L_CHUNKS[k - 1]
 
             def group(g, carry):
@@ -336,6 +335,22 @@
     others(rsend, rrecv, TILE).wait_send()
     others(lsend, rrecv, TILE).wait_send()
     others(psend, rrecv, TILE).wait_send()
+    pltpu.make_async_remote_copy(
+        src_ref=prod.at[mine],
+        dst_ref=prod.at[mine],
+        send_sem=qsend,
+        recv_sem=rrecv,
+        device_id=partner,
+        device_id_type=LOGICAL,
+    ).wait_send()
+    pltpu.make_async_remote_copy(
+        src_ref=pair,
+        dst_ref=whole.at[mine],
+        send_sem=xsend,
+        recv_sem=rrecv,
+        device_id=partner,
+        device_id_type=LOGICAL,
+    ).wait_send()
 
 
 def body(pair_acts, residue_mask, norm_in_gain, w_proj, norm_out_gain, w_out):
@@ -367,17 +382,17 @@
             pltpu.VMEM((64, TILE, TILE), BF16),
             pltpu.VMEM((CHANNELS, TILE, TILE), BF16),
             dma((len(X_CHUNKS),)),
+            dma,
             dma((len(X_CHUNKS),)),
-            dma((len(X_CHUNKS),)),
             dma,
             dma,
             dma,
             dma((parts,)),
             dma,
             dma((parts,)),
+            dma,
             dma((parts,)),
-            dma((parts,)),
-            dma((3, parts)),
+            dma((3,)),
             dma((6,)),
             pltpu.SemaphoreType.REGULAR,
             pltpu.SemaphoreType.REGULAR,

time: 86.4 us -> 85.9 us (level)
  no operation moved by 1% of the time
where the time goes in v7:
time: 85.9 us; the launch traced here: 85.8 us
  Pallas kernels  84.5 us (98%)
  local copies, waits for them, and re-layouts  1.32 us (2%)
    pallas_call x1, Pallas kernels, body(): pl.pallas_call(kernel, out_shape=pltpu.VMEM((OWN, TILE, TILE), BF16), in_...  84.5 us

profile of v7, /device:TPU:1, one launch (start us, length us, event | category | flops | bytes accessed | tf_op | source)
XLA Modules:
  0.0 85.8 jit_solution(5136636064321097392)
XLA Ops:
  0.0 84.5 %triangle.1 = bf16[64,128,128]{2,1,0:T(8,128)(2,1)S(1)} custom-call(bf16[64,128,128]{2,1,0:T(8,128)(2,1)} %pair.1, s32[1024]{0:T(1024)} %mask_hbm.1, f32[128]{0:T(128)} %gain_in_hbm.1, f32[128]{0:T(128)} %gain_out_hbm.1, s32[8,128]{1,0:T(8,128)} %bitcast.3, bf16[320,128]{1,0:T(8,128)(2,1)} %bitcast.2, bf16[64,128]{1,0:T(8,128)(2,1)} %w_out_hbm.1), custom_call_target="tpu_custom_call" | custom-call | tf_op jit(solution)/shard_map/triangle/pallas_call | solution.py:360
  84.5 1.3 %copy.8 = bf16[64,128,128]{2,1,0:T(8,128)(2,1)} copy(bf16[64,128,128]{2,1,0:T(8,128)(2,1)S(1)} %triangle.1) | data formatting | bytes 4194304

commit v8 on v7

--- a/solution.py
+++ b/solution.py
@@ -14,7 +14,7 @@
 GROUP = 16
 BLOCK = 8
 X_CHUNKS = ((0, 16), (16, 48), (64, 64))
-R_CHUNKS = ((0, 16), (16, 16), (32, 16), (48, 16), (64, 32), (96, 32))
+R_CHUNKS = ((0, 16), (16, 16), (32, 16), (48, 16), (64, 16), (80, 16), (96, 16), (112, 16))
 L_CHUNKS = ((0, 32), (32, 32), (64, 16), (80, 16), (96, 16), (112, 16))
 INNER = [(1, 2), (2, 1), (3, 3), (0, 1), (1, 0), (3, 2), (2, 3), (0, 2), (2, 0), (1, 1), (3, 1), (1, 3), (0, 3), (3, 0), (2, 2), (0, 0)]
 

time: 85.9 us -> 85.9 us (level)
  no operation moved by 1% of the time
where the time goes in v8:
time: 85.9 us; the launch traced here: 85.8 us
  Pallas kernels  84.5 us (98%)
  local copies, waits for them, and re-layouts  1.32 us (2%)
    pallas_call x1, Pallas kernels, body(): pl.pallas_call(kernel, out_shape=pltpu.VMEM((OWN, TILE, TILE), BF16), in_...  84.5 us

profile of v8, /device:TPU:1, one launch (start us, length us, event | category | flops | bytes accessed | tf_op | source)
XLA Modules:
  0.0 85.8 jit_solution(1422348782688954150)
XLA Ops:
  0.0 84.5 %triangle.1 = bf16[64,128,128]{2,1,0:T(8,128)(2,1)S(1)} custom-call(bf16[64,128,128]{2,1,0:T(8,128)(2,1)} %pair.1, s32[1024]{0:T(1024)} %mask_hbm.1, f32[128]{0:T(128)} %gain_in_hbm.1, f32[128]{0:T(128)} %gain_out_hbm.1, s32[8,128]{1,0:T(8,128)} %bitcast.3, bf16[320,128]{1,0:T(8,128)(2,1)} %bitcast.2, bf16[64,128]{1,0:T(8,128)(2,1)} %w_out_hbm.1), custom_call_target="tpu_custom_call" | custom-call | tf_op jit(solution)/shard_map/triangle/pallas_call | solution.py:360
  84.5 1.3 %copy.8 = bf16[64,128,128]{2,1,0:T(8,128)(2,1)} copy(bf16[64,128,128]{2,1,0:T(8,128)(2,1)S(1)} %triangle.1) | data formatting | bytes 4194304

commit v9 on v7

--- a/solution.py
+++ b/solution.py
@@ -353,11 +353,26 @@
     ).wait_send()
 
 
+STORES = 4
+
+
+def store_kernel(result, out, sems):
+    size = OWN // STORES
+    copies = [
+        pltpu.make_async_copy(result.at[pl.ds(k * size, size)], out.at[pl.ds(k * size, size)], sems.at[k])
+        for k in range(STORES)
+    ]
+    for copy in copies:
+        copy.start()
+    for copy in copies:
+        copy.wait()
+
+
 def body(pair_acts, residue_mask, norm_in_gain, w_proj, norm_out_gain, w_out):
     vmem = pl.BlockSpec(memory_space=pltpu.VMEM)
     dma = pltpu.SemaphoreType.DMA
     parts = len(L_CHUNKS)
-    return pl.pallas_call(
+    result = pl.pallas_call(
         kernel,
         out_shape=pltpu.VMEM((OWN, TILE, TILE), BF16),
         in_specs=[pl.BlockSpec(memory_space=pl.ANY)] * 7,
@@ -408,6 +423,15 @@
         w_proj.reshape(5 * OWN, CHANNELS),
         w_out,
     )
+    return pl.pallas_call(
+        store_kernel,
+        out_shape=jax.ShapeDtypeStruct((OWN, TILE, TILE), BF16),
+        in_specs=[vmem],
+        out_specs=pl.BlockSpec(memory_space=pl.ANY),
+        scratch_shapes=[dma((STORES,))],
+        compiler_params=pltpu.CompilerParams(vmem_limit_bytes=8 << 20),
+        name="store",
+    )(result)
 
 
 def solution(mesh):

time: 85.9 us -> 85.9 us (level)
  local copies, waits for them, and re-layouts: 1.32 us -> 0 us
  Pallas kernels: 84.5 us -> 85.8 us
    pallas_call x0 -> x1, Pallas kernels: none -> 1.35 us  [body(): pl.pallas_call(store_kernel, out_shape=jax.ShapeDtypeStruct((OWN, TILE, T...]
    unnamed x1 -> x0, local copies, waits for them, and re-layouts: 1.32 us -> none
where the time goes in v9:
time: 85.9 us; the launch traced here: 85.8 us
  Pallas kernels  85.8 us (100%)
    pallas_call x1, Pallas kernels, body(): pl.pallas_call(kernel, out_shape=pltpu.VMEM((OWN, TILE, TILE), BF16), in_...  84.5 us

profile of v9, /device:TPU:1, one launch (start us, length us, event | category | flops | bytes accessed | tf_op | source)
XLA Modules:
  0.0 85.8 jit_solution(10694480448816054228)
XLA Ops:
  0.0 84.5 %triangle.1.result = bf16[64,128,128]{2,1,0:T(8,128)(2,1)S(1)} custom-call(bf16[64,128,128]{2,1,0:T(8,128)(2,1)} %pair.1, s32[1024]{0:T(1024)} %mask_hbm.1, f32[128]{0:T(128)} %gain_in_hbm.1, f32[128]{0:T(128)} %gain_out_hbm.1, s32[8,128]{1,0:T(8,128)} %bitcast.3, bf16[320,128]{1,0:T(8,128)(2,1)} %bitcast.2, bf16[64,128]{1,0:T(8,128)(2,1)} %w_out_hbm.1), custom_call_target="tpu_custom_call" | custom-call | tf_op jit(solution)/shard_map/triangle/pallas_call | solution.py:375
  84.5 1.3 %store.1 = bf16[64,128,128]{2,1,0:T(8,128)(2,1)} custom-call(bf16[64,128,128]{2,1,0:T(8,128)(2,1)S(1)} %triangle.1.result), custom_call_target="tpu_custom_call" | custom-call | tf_op jit(solution)/shard_map/store/pallas_call | solution.py:426
